TPU v7x, 256 devices: a whole 4x4x8 slice. The times are simulated.
256 devices in a mesh: energy: 64 (over x, z_hi, y), space: 4 (over z_lo, core).
Axes of the slice: x: 4, y: 4, z: 8 (z_hi: 4, z_lo: 2; z = z_hi * 2 + z_lo), core: 2. Of those that a mesh axis runs over, the one named last changes fastest.
Arguments:
- g_lesser: bfloat16 [64, 2, 4, 512, 512], P('energy', None, 'space'), may hold values from -6 to 6, as said below
- w_lesser: bfloat16 [64, 2, 4, 512, 512], P('energy', None, 'space'), may hold values from -6 to 6, as said below
- g_retarded: bfloat16 [64, 2, 4, 4, 512, 512], P('energy', None, 'space'), may hold values from -0.1875 to 0.1875
- energy_index: int32 [64], replicated, may hold values from 0 to 63, each once
Outputs:
- sigma_lesser: bfloat16 [64, 2, 4, 512, 512], P('energy', None, 'space')
- delta_green: bfloat16 [64, 2, 4, 512, 512], P('energy', None, 'space')
Inputs may be any that keep to these rules, and one draw needn't show every extreme that they name: `g_lesser`: anti-Hermitian in every diagonal block at every energy: element (j, i) of component 0 is minus element (i, j), of component 1 equal to it. `w_lesser`: anti-Hermitian in every diagonal block at every energy: element (j, i) of component 0 is minus element (i, j), of component 1 equal to it. `energy_index`: each grid point once.
All inputs are finite; a program needn't handle non-finite values.
Results may differ from a plain program's by a relative error of at most 0.013.
Values may be sent and summed in bfloat16 or wider, within the bound.
A program may use at most 128 MiB of HBM per device.

v0:
```python
import math
import jax
import jax.numpy as jnp
from jax import lax
from jax.sharding import PartitionSpec as P


def twiddles(energy_index, per_device, groups):
    grid_size = energy_index.shape[0]
    padded_len = 2 * grid_size
    row_count = 2 * grid_size
    row_ids = lax.iota(jnp.int32, row_count)
    local_energy = row_ids // (2 * groups)
    component = row_ids // groups % 2
    source = row_ids % groups
    stored = source * per_device + local_energy
    grid_point = energy_index[stored]
    frequency = lax.iota(jnp.int32, padded_len)
    forward_phase = frequency[:, None] * grid_point[None, :] % padded_len
    forward_angle = forward_phase.astype(jnp.float32) * (2.0 * math.pi / padded_len)
    cos_fwd = jnp.cos(forward_angle)
    sin_fwd = jnp.sin(forward_angle)
    real_column = (component == 0)[None, :]
    forward = jnp.concatenate(
        [jnp.where(real_column, cos_fwd, sin_fwd), jnp.where(real_column, -sin_fwd, cos_fwd)],
        axis=0,
    )
    shifted = grid_point + grid_size // 2
    backward_phase = shifted[:, None] * frequency[None, :] % padded_len
    backward_angle = backward_phase.astype(jnp.float32) * (2.0 * math.pi / padded_len)
    cos_back = jnp.cos(backward_angle)
    sin_back = jnp.sin(backward_angle)
    real_row = (component == 0)[:, None]
    factor = grid_size ** (-0.5) / padded_len
    left_half = jnp.where(real_row, -sin_back, cos_back) * factor
    right_half = jnp.where(real_row, -cos_back, -sin_back) * factor
    backward = jnp.concatenate([left_half, right_half], axis=1)
    return (forward, backward)


def transform(matrix_high, matrix_low, operand):
    return jnp.dot(matrix_high, operand, preferred_element_type=jnp.float32) + jnp.dot(
        matrix_low, operand, preferred_element_type=jnp.float32
    )


def convolve(green_rows, screen_rows, forward, backward):
    padded_len = forward.shape[0] // 2
    forward_high = forward.astype(jnp.bfloat16)
    forward_low = (forward - forward_high.astype(jnp.float32)).astype(jnp.bfloat16)
    green_hat = transform(forward_high, forward_low, green_rows)
    screen_hat = transform(forward_high, forward_low, screen_rows)
    green_real = green_hat[:padded_len]
    green_imag = green_hat[padded_len:]
    screen_real = screen_hat[:padded_len]
    screen_imag = screen_hat[padded_len:]
    prod_real = green_real * screen_real - green_imag * screen_imag
    prod_imag = green_real * screen_imag + green_imag * screen_real
    merged = jnp.concatenate([prod_real, prod_imag], axis=0)
    return jnp.dot(backward, merged, precision=lax.Precision.HIGH).astype(jnp.bfloat16)


def shards(g_lesser, w_lesser, g_retarded, energy_index):
    energies_here = g_lesser.shape[0]
    width = g_lesser.shape[3]
    groups = lax.axis_size("energy")
    forward, backward = twiddles(energy_index, energies_here, groups)
    own_row = g_retarded[:, :, 0]
    columns = width * width // groups
    green = g_lesser.reshape(energies_here, 2, groups, columns)
    screen = w_lesser.reshape(energies_here, 2, groups, columns)
    green_el, screen_el = (
        lax.all_to_all(green, "energy", split_axis=2, concat_axis=2, tiled=True),
        lax.all_to_all(screen, "energy", split_axis=2, concat_axis=2, tiled=True),
    )
    sigma_el = convolve(
        green_el.reshape(-1, columns), screen_el.reshape(-1, columns), forward, backward
    )
    sigma_el = sigma_el.reshape(energies_here, 2, groups, columns)
    sigma_back = lax.all_to_all(sigma_el, "energy", split_axis=2, concat_axis=2, tiled=True)
    sigma_lesser = sigma_back.reshape(energies_here, 2, 1, width, width)
    first_prod = jnp.einsum(
        "ecnij,ednjl->encdil",
        own_row,
        lax.all_gather(sigma_lesser, "space", axis=2, tiled=True),
        preferred_element_type=jnp.float32,
    )
    left_product = jnp.stack(
        [
            first_prod[:, :, 0, 0] - first_prod[:, :, 1, 1],
            first_prod[:, :, 0, 1] + first_prod[:, :, 1, 0],
        ],
        axis=1,
    ).astype(jnp.bfloat16)
    second_prod = jnp.einsum(
        "ecnil,ednml->ecdim", left_product, own_row, preferred_element_type=jnp.float32
    )
    out_real = second_prod[:, 0, 0] + second_prod[:, 1, 1]
    out_imag = second_prod[:, 1, 0] - second_prod[:, 0, 1]
    delta = jnp.stack([out_real, out_imag], axis=1)
    delta_green = delta.astype(jnp.bfloat16).reshape(energies_here, 2, 1, width, width)
    return (sigma_lesser, delta_green)


def solution(mesh):
    return jax.shard_map(
        shards,
        mesh=mesh,
        in_specs=(
            P("energy", None, "space", None, None),
            P("energy", None, "space", None, None),
            P("energy", None, "space", None, None, None),
            P(),
        ),
        out_specs=(P("energy", None, "space", None, None), P("energy", None, "space", None, None)),
        check_vma=False,
    )
```

profile of v0, /device:TPU:1, one launch (start us, length us, event | category | flops | bytes accessed | tf_op | source)
XLA Modules:
  0.0 215.1 jit_solution(1046797866290290498)
XLA Ops:
  7.2 0.0 copy-start
  7.2 0.0 copy-start.4
  7.2 1.6 reshape.274
  8.8 2.1 copy.28
  10.9 15.1 %all-to-all-start.1 = ((bf16[1,2,64,4096]{3,1,0,2:T(2,128)(2,1)}), bf16[1,2,64,4096]{3,1,0,2:T(2,128)(2,1)S(1)}, u32[]{:S(2)}, u32[]{:S(2)}) async-start(bf16[1,2,64,4096]{3,1,0,2:T(2,128)(2,1)} %copy.28), calls=%async_computation.1 | async-start | bytes 2097152 | tf_op jit(solution)/shard_map/all_to_all | solution.py:74
  26.0 0.0 copy-done.4
  26.0 0.5 reshape.272
  26.6 2.1 copy.26
  28.6 25.1 %all-to-all-done.1 = bf16[1,2,64,4096]{3,1,0,2:T(2,128)(2,1)S(1)} async-done(((bf16[1,2,64,4096]{3,1,0,2:T(2,128)(2,1)}), bf16[1,2,64,4096]{3,1,0,2:T(2,128)(2,1)S(1)}, u32[]{:S(2)}, u32[]{:S(2)}) %all-to-all-start.1) | async-done | bytes 1048608 | tf_op jit(solution)/shard_map/all_to_all | solution.py:74
  53.7 8.3 %all-to-all-start = ((bf16[1,2,64,4096]{3,1,0,2:T(2,128)(2,1)}), bf16[1,2,64,4096]{3,1,0,2:T(2,128)(2,1)S(1)}, u32[]{:S(2)}, u32[]{:S(2)}) async-start(bf16[1,2,64,4096]{3,1,0,2:T(2,128)(2,1)} %copy.26), calls=%async_computation | async-start | bytes 2097152 | tf_op jit(solution)/shard_map/all_to_all | solution.py:73
  62.0 0.2 all-gather.2.cloned.1.call-start
  62.3 0.0 copy-done
  62.3 1.2 gather_fusion
  63.6 0.6 select_multiply_fusion.1
  64.2 0.6 copy.29
  64.8 0.7 fusion.36
  65.5 2.6 %convolution_add_fusion = f32[256,4096]{1,0:T(8,128)} fusion(f32[256,4096]{1,0:T(8,128)S(1)} %fusion.36, bf16[128,4096]{1,0:T(8,128)(2,1)S(1)} %bitcast.74, f32[128,128]{1,0:T(8,128)S(1)} %get-tuple-element.18, f32[128,128]{1,0:T(8,128)S(1)} %get-tuple-element.19), kind=kOutput, calls=%fused_computation.2 | convolution fusion | flops 269647872 | bytes 9568256 | tf_op jit(solution)/shard_map/dot_general | solution.py:42
  68.1 22.7 %all-to-all-done = bf16[1,2,64,4096]{3,1,0,2:T(2,128)(2,1)S(1)} async-done(((bf16[1,2,64,4096]{3,1,0,2:T(2,128)(2,1)}), bf16[1,2,64,4096]{3,1,0,2:T(2,128)(2,1)S(1)}, u32[]{:S(2)}, u32[]{:S(2)}) %all-to-all-start) | async-done | bytes 1048608 | tf_op jit(solution)/shard_map/all_to_all | solution.py:73
  90.8 0.6 copy.27
  91.3 0.7 fusion.38
  92.0 0.0 copy-start.2
  92.0 0.7 convolution_add_fusion.1
  92.8 1.5 copy-done.2
  94.2 0.9 multiply_subtract_fusion
  95.2 1.5 convolution_convert_fusion
  96.7 1.1 copy.30
  97.8 32.1 %all_to_all.15 = bf16[1,2,64,4096]{3,1,0,2:T(2,128)(2,1)S(1)} all-to-all(bf16[1,2,64,4096]{3,1,0,2:T(2,128)(2,1)S(1)} %copy.30), channel_id=1, replica_groups=mesh['energy'=64,'space'=4] {'energy'}, dimensions={2} | all-to-all | bytes 2097152 | tf_op jit(solution)/shard_map/all_to_all | solution.py:80
  130.0 0.6 copy.31
  130.6 1.3 reshape.277
  131.9 0.0 all-gather.2.cloned.1.call-update
  131.9 47.4 %all-gather.2.cloned.1.call-done = bf16[1,2,4,512,512]{4,3,1,0,2:T(8,128)(2,1)} async-done(((bf16[1,2,1,512,512]{4,3,1,0,2:T(8,128)(2,1)}), bf16[1,2,4,512,512]{4,3,1,0,2:T(8,128)(2,1)}) %all-gather.2.cloned.1.call-update) | async-done | bytes 4194320 | tf_op jit(solution)/shard_map/all_gather | solution.py:85
  179.3 14.1 %convolution_bitcast_fusion = f32[1,4,2,2,512,512]{4,5,2,3,1,0:T(8,128)} fusion(bf16[1,2,4,512,512]{4,3,1,0,2:T(8,128)(2,1)} %all-gather.2.cloned.1.call-done, bf16[1,2,1,4,512,512]{5,4,3,2,1,0:T(8,128)(2,1)} %param.6), kind=kOutput, calls=%fused_computation.1 | convolution fusion | flops 4294967296 | bytes 25165824 | tf_op jit(solution)/shard_map/ecnij,ednjl->encdil/dot_general | solution.py:82
  193.4 4.2 %fusion.13 = bf16[1,4,512,512]{2,3,1,0:T(8,128)(2,1)S(1)} fusion(f32[1,4,2,2,512,512]{4,5,2,3,1,0:T(8,128)} %convolution_bitcast_fusion), kind=kLoop, calls=%fused_computation.22 | loop fusion | flops 2097152 | bytes 10485760 | tf_op jit(solution)/shard_map/add | solution.py:91
  197.6 0.0 copy-start.3
  197.6 4.4 %fusion.12 = bf16[1,4,512,512]{2,3,1,0:T(8,128)(2,1)S(1)} fusion(f32[1,4,2,2,512,512]{4,5,2,3,1,0:T(8,128)} %convolution_bitcast_fusion), kind=kLoop, calls=%fused_computation.21 | loop fusion | flops 2097152 | bytes 10485760 | tf_op jit(solution)/shard_map/sub | solution.py:90
  202.1 0.2 copy-done.3
  202.3 0.0 copy-start.1
  202.3 4.5 %fusion.11 = f32[1,2,2,512,512]{4,3,2,1,0:T(8,128)S(1)} fusion(bf16[1,4,512,512]{2,3,1,0:T(8,128)(2,1)S(1)} %fusion.13, bf16[1,4,512,512]{2,3,1,0:T(8,128)(2,1)S(1)} %fusion.12, bf16[1,2,1,4,512,512]{5,4,3,2,1,0:T(8,128)(2,1)S(1)} %copy-done.3), kind=kOutput, calls=%fused_computation.20 | convolution fusion | flops 4303355904 | bytes 12582912 | tf_op jit(solution)/shard_map/ecnil,ednml->ecdim/dot_general | solution.py:95
  206.8 0.4 fusion.15
  207.2 1.1 pad_maximum_fusion
  208.2 0.0 copy-done.1
  (4 shorter events, 0.0 us)
Async XLA Ops:
  7.2 55.1 %copy-start = (s32[64]{0:T(128)S(1)}, s32[64]{0:T(128)}, u32[]{:S(2)}) copy-start(s32[64]{0:T(128)} %param.7) | copy-start | bytes 772
  7.2 18.8 %copy-start.4 = (bf16[1,2,1,512,512]{4,3,2,1,0:T(8,128)(2,1)S(1)}, bf16[1,2,1,512,512]{4,3,2,1,0:T(8,128)(2,1)}, u32[]{:S(2)}) copy-start(bf16[1,2,1,512,512]{4,3,2,1,0:T(8,128)(2,1)} %param.4) | copy-start | bytes 3145732
  10.9 42.8 %all-to-all-start.1 = ((bf16[1,2,64,4096]{3,1,0,2:T(2,128)(2,1)}), bf16[1,2,64,4096]{3,1,0,2:T(2,128)(2,1)S(1)}, u32[]{:S(2)}, u32[]{:S(2)}) async-start(bf16[1,2,64,4096]{3,1,0,2:T(2,128)(2,1)} %copy.28), calls=%async_computation.1 | async-start | bytes 2097152 | tf_op jit(solution)/shard_map/all_to_all | solution.py:74
  53.7 37.0 %all-to-all-start = ((bf16[1,2,64,4096]{3,1,0,2:T(2,128)(2,1)}), bf16[1,2,64,4096]{3,1,0,2:T(2,128)(2,1)S(1)}, u32[]{:S(2)}, u32[]{:S(2)}) async-start(bf16[1,2,64,4096]{3,1,0,2:T(2,128)(2,1)} %copy.26), calls=%async_computation | async-start | bytes 2097152 | tf_op jit(solution)/shard_map/all_to_all | solution.py:73
  62.0 117.3 %all-gather.2.cloned.1.call-start = ((), (), s32[]{:S(2)}) async-start(), calls=%async_computation.3 | async-start | bytes 5242880 | tf_op jit(solution)/shard_map/all_gather | solution.py:85
  92.0 2.2 %copy-start.2 = (f32[256,4096]{1,0:T(8,128)S(1)}, f32[256,4096]{1,0:T(8,128)}, u32[]{:S(2)}) copy-start(f32[256,4096]{1,0:T(8,128)} %convolution_add_fusion) | copy-start | bytes 12582916
  197.6 4.6 %copy-start.3 = (bf16[1,2,1,4,512,512]{5,4,3,2,1,0:T(8,128)(2,1)S(1)}, bf16[1,2,1,4,512,512]{5,4,3,2,1,0:T(8,128)(2,1)}, u32[]{:S(2)}) copy-start(bf16[1,2,1,4,512,512]{5,4,3,2,1,0:T(8,128)(2,1)} %param.6) | copy-start | bytes 12582916
  202.3 6.0 %copy-start.1 = (s32[64]{0:T(128)S(1)}, s32[64]{0:T(128)}, u32[]{:S(2)}) copy-start(s32[64]{0:T(128)} %param.7) | copy-start | bytes 772
Sparse Core Ops, SparseCore 0:
  132.0 47.2 all-gather.1
where the time goes:
time: 215 us
  waiting for transfers between devices  95.2 us (44%)
  blocking collectives  32.1 us (15%)
  matrix products  24.9 us (12%)
  starting transfers between devices  23.7 us (11%)
  between operations  14.2 us (7%)
  local copies, waits for them, and re-layouts  13.4 us (6%)
  other arithmetic  11.6 us (5%)
    all_gather x1, waiting for transfers between devices, shards(): lax.all_gather(sigma_lesser, 'space', axis=2, tiled=True)  47.4 us
    all_to_all x1, blocking collectives, shards(): lax.all_to_all(sigma_el, 'energy', split_axis=2, concat_axis=2, tiled=True)  32.1 us
    all_to_all x1, waiting for transfers between devices, shards(): lax.all_to_all(screen, 'energy', split_axis=2, concat_axis=2, tiled=True)  25.1 us
    all_to_all x1, waiting for transfers between devices, shards(): lax.all_to_all(green, 'energy', split_axis=2, concat_axis=2, tiled=True)  22.7 us
    all_to_all x1, starting transfers between devices, shards(): lax.all_to_all(screen, 'energy', split_axis=2, concat_axis=2, tiled=True)  15.1 us
    dot_general x1, matrix products, shards(): jnp.einsum('ecnij,ednjl->encdil', own_row, lax.all_gather(sigma_lesser, '...  14.1 us
    all_to_all x1, starting transfers between devices, shards(): lax.all_to_all(green, 'energy', split_axis=2, concat_axis=2, tiled=True)  8.33 us
    dot_general x1, matrix products, shards(): jnp.einsum('ecnil,ednml->ecdim', left_product, own_row, preferred_element...  4.54 us
  transfers between devices with their start and end apart: 3, of which 3 were waited for; matrix products, arithmetic and copies ran while one was open for 4% of the time, Pallas kernels for 0%

commit v1 on v0

--- a/solution.py
+++ b/solution.py
@@ -82,7 +82,7 @@
     first_prod = jnp.einsum(
         "ecnij,ednjl->encdil",
         own_row,
-        lax.all_gather(sigma_lesser, "space", axis=2, tiled=True),
+        jnp.concatenate(lax.all_gather(sigma_lesser, "space"), axis=2),
         preferred_element_type=jnp.float32,
     )
     left_product = jnp.stack(

time: 215 us -> 211 us (0.981)
  local copies, waits for them, and re-layouts: 13.4 us -> 23.1 us
  other arithmetic: 11.6 us -> 4.62 us
  matrix products: 24.9 us -> 18.4 us
    all_gather x0 -> x1, local copies, waits for them, and re-layouts: none -> 7.33 us  [shards(): lax.all_gather(sigma_lesser, 'space')]
    dot_general x1, matrix products: 14.1 us -> 7.61 us  [shards(): jnp.einsum('ecnij,ednjl->encdil', own_row, jnp.concatenate(lax.all_gather...]
    sub x1, other arithmetic: 4.42 us -> 0.89 us  [shards(): first_prod[:, :, 0, 0] - first_prod[:, :, 1, 1]]
    add x1, other arithmetic: 4.19 us -> 0.75 us  [shards(): first_prod[:, :, 0, 1] + first_prod[:, :, 1, 0]]
  transfers between devices with their start and end apart: 3 -> 3, of which waited for: 3 -> 3; matrix products, arithmetic and copies ran while one was open for 4% -> 5% of each run, Pallas kernels for 0% -> 0%
where the time goes in v1:
time: 211 us; the launch traced here: 210 us
  waiting for transfers between devices  93.9 us (45%)
  blocking collectives  32.1 us (15%)
  starting transfers between devices  23.7 us (11%)
  local copies, waits for them, and re-layouts  23.1 us (11%)
  matrix products  18.4 us (9%)
  between operations  14.2 us (7%)
  other arithmetic  4.62 us (2%)
    all_gather x1, waiting for transfers between devices, shards(): lax.all_gather(sigma_lesser, 'space')  46.1 us
    all_to_all x1, blocking collectives, shards(): lax.all_to_all(sigma_el, 'energy', split_axis=2, concat_axis=2, tiled=True)  32.1 us
    all_to_all x1, waiting for transfers between devices, shards(): lax.all_to_all(screen, 'energy', split_axis=2, concat_axis=2, tiled=True)  25.1 us
    all_to_all x1, waiting for transfers between devices, shards(): lax.all_to_all(green, 'energy', split_axis=2, concat_axis=2, tiled=True)  22.7 us
    all_to_all x1, starting transfers between devices, shards(): lax.all_to_all(screen, 'energy', split_axis=2, concat_axis=2, tiled=True)  15.1 us
    all_to_all x1, starting transfers between devices, shards(): lax.all_to_all(green, 'energy', split_axis=2, concat_axis=2, tiled=True)  8.33 us
    dot_general x1, matrix products, shards(): jnp.einsum('ecnij,ednjl->encdil', own_row, jnp.concatenate(lax.all_gather...  7.61 us
    all_gather x1, local copies, waits for them, and re-layouts, shards(): lax.all_gather(sigma_lesser, 'space')  7.33 us
  transfers between devices with their start and end apart: 3, of which 3 were waited for; matrix products, arithmetic and copies ran while one was open for 5% of the time, Pallas kernels for 0%

profile of v1, /device:TPU:1, one launch (start us, length us, event | category | flops | bytes accessed | tf_op | source)
XLA Modules:
  0.0 210.1 jit_solution(10122084408845452529)
XLA Ops:
  7.2 0.0 copy-start
  7.2 0.0 copy-start.4
  7.2 1.6 reshape.279
  8.8 2.1 copy.25
  10.9 15.1 %all-to-all-start.1 = ((bf16[1,2,64,4096]{3,1,0,2:T(2,128)(2,1)}), bf16[1,2,64,4096]{3,1,0,2:T(2,128)(2,1)S(1)}, u32[]{:S(2)}, u32[]{:S(2)}) async-start(bf16[1,2,64,4096]{3,1,0,2:T(2,128)(2,1)} %copy.25), calls=%async_computation.1 | async-start | bytes 2097152 | tf_op jit(solution)/shard_map/all_to_all | solution.py:74
  26.0 0.0 copy-done.4
  26.0 0.5 reshape.277
  26.6 2.1 copy.23
  28.6 25.1 %all-to-all-done.1 = bf16[1,2,64,4096]{3,1,0,2:T(2,128)(2,1)S(1)} async-done(((bf16[1,2,64,4096]{3,1,0,2:T(2,128)(2,1)}), bf16[1,2,64,4096]{3,1,0,2:T(2,128)(2,1)S(1)}, u32[]{:S(2)}, u32[]{:S(2)}) %all-to-all-start.1) | async-done | bytes 1048608 | tf_op jit(solution)/shard_map/all_to_all | solution.py:74
  53.7 8.3 %all-to-all-start = ((bf16[1,2,64,4096]{3,1,0,2:T(2,128)(2,1)}), bf16[1,2,64,4096]{3,1,0,2:T(2,128)(2,1)S(1)}, u32[]{:S(2)}, u32[]{:S(2)}) async-start(bf16[1,2,64,4096]{3,1,0,2:T(2,128)(2,1)} %copy.23), calls=%async_computation | async-start | bytes 2097152 | tf_op jit(solution)/shard_map/all_to_all | solution.py:73
  62.0 0.2 all-gather.2.cloned.1.call-start
  62.3 0.0 copy-done
  62.3 1.2 gather_fusion
  63.6 0.6 select_multiply_fusion.1
  64.2 0.6 copy.26
  64.8 0.7 fusion.36
  65.5 2.6 %convolution_add_fusion = f32[256,4096]{1,0:T(8,128)} fusion(f32[256,4096]{1,0:T(8,128)S(1)} %fusion.36, bf16[128,4096]{1,0:T(8,128)(2,1)S(1)} %bitcast.78, f32[128,128]{1,0:T(8,128)S(1)} %get-tuple-element.12, f32[128,128]{1,0:T(8,128)S(1)} %get-tuple-element.13), kind=kOutput, calls=%fused_computation.2 | convolution fusion | flops 269647872 | bytes 9568256 | tf_op jit(solution)/shard_map/dot_general | solution.py:42
  68.1 22.7 %all-to-all-done = bf16[1,2,64,4096]{3,1,0,2:T(2,128)(2,1)S(1)} async-done(((bf16[1,2,64,4096]{3,1,0,2:T(2,128)(2,1)}), bf16[1,2,64,4096]{3,1,0,2:T(2,128)(2,1)S(1)}, u32[]{:S(2)}, u32[]{:S(2)}) %all-to-all-start) | async-done | bytes 1048608 | tf_op jit(solution)/shard_map/all_to_all | solution.py:73
  90.8 0.6 copy.24
  91.3 0.7 fusion.38
  92.0 0.0 copy-start.2
  92.0 0.7 convolution_add_fusion.1
  92.8 1.5 copy-done.2
  94.2 0.9 multiply_subtract_fusion
  95.2 1.5 convolution_convert_fusion
  96.7 1.1 copy.27
  97.8 32.1 %all_to_all.15 = bf16[1,2,64,4096]{3,1,0,2:T(2,128)(2,1)S(1)} all-to-all(bf16[1,2,64,4096]{3,1,0,2:T(2,128)(2,1)S(1)} %copy.27), channel_id=1, replica_groups=mesh['energy'=64,'space'=4] {'energy'}, dimensions={2} | all-to-all | bytes 2097152 | tf_op jit(solution)/shard_map/all_to_all | solution.py:80
  130.0 0.6 copy.28
  130.6 1.3 all_gather_reshape.3
  131.9 0.0 all-gather.2.cloned.1.call-update
  131.9 1.3 reshape.282
  133.2 46.1 %all-gather.2.cloned.1.call-done = bf16[4,1,2,1,512,512]{5,4,3,2,1,0:T(8,128)(2,1)} async-done(((bf16[1,1,2,1,512,512]{5,4,3,2,1,0:T(8,128)(2,1)}), bf16[4,1,2,1,512,512]{5,4,3,2,1,0:T(8,128)(2,1)}) %all-gather.2.cloned.1.call-update) | async-done | bytes 4194320 | tf_op jit(solution)/shard_map/all_gather | solution.py:85
  179.3 7.3 %copy.31 = bf16[4,1,2,1,512,512]{4,5,2,0,3,1:T(8,128)(2,1)} copy(bf16[4,1,2,1,512,512]{5,4,3,2,1,0:T(8,128)(2,1)} %all-gather.2.cloned.1.call-done) | data formatting | bytes 8388608 | tf_op jit(solution)/shard_map/all_gather | solution.py:85
  186.7 7.6 %convolution_bitcast_fusion = f32[1,4,2,2,512,512]{4,5,2,3,1,0:T(8,128)S(1)} fusion(bf16[4,1,2,1,512,512]{4,5,2,0,3,1:T(8,128)(2,1)} %copy.31, bf16[1,2,1,4,512,512]{5,4,3,2,1,0:T(8,128)(2,1)} %param.6), kind=kOutput, calls=%fused_computation.1 | convolution fusion | flops 4294967296 | bytes 25165824 | tf_op jit(solution)/shard_map/ecnij,ednjl->encdil/dot_general | solution.py:82
  194.3 0.8 fusion.13
  195.0 0.0 copy-start.3
  195.0 0.9 fusion.12
  195.9 1.3 copy-done.3
  197.2 0.0 copy-start.1
  197.2 4.5 %fusion.11 = f32[1,2,2,512,512]{4,3,2,1,0:T(8,128)S(1)} fusion(bf16[1,4,512,512]{2,3,1,0:T(8,128)(2,1)S(1)} %fusion.13, bf16[1,4,512,512]{2,3,1,0:T(8,128)(2,1)S(1)} %fusion.12, bf16[1,2,1,4,512,512]{5,4,3,2,1,0:T(8,128)(2,1)S(1)} %copy-done.3), kind=kOutput, calls=%fused_computation.20 | convolution fusion | flops 4303355904 | bytes 12582912 | tf_op jit(solution)/shard_map/ecnil,ednml->ecdim/dot_general | solution.py:95
  201.8 0.4 fusion.15
  202.1 1.1 pad_maximum_fusion
  203.2 0.0 copy-done.1
  (4 shorter events, 0.0 us)
Async XLA Ops:
  7.2 55.1 %copy-start = (s32[64]{0:T(128)S(1)}, s32[64]{0:T(128)}, u32[]{:S(2)}) copy-start(s32[64]{0:T(128)} %param.7) | copy-start | bytes 772
  7.2 18.8 %copy-start.4 = (bf16[1,2,1,512,512]{4,3,2,1,0:T(8,128)(2,1)S(1)}, bf16[1,2,1,512,512]{4,3,2,1,0:T(8,128)(2,1)}, u32[]{:S(2)}) copy-start(bf16[1,2,1,512,512]{4,3,2,1,0:T(8,128)(2,1)} %param.4) | copy-start | bytes 3145732
  10.9 42.8 %all-to-all-start.1 = ((bf16[1,2,64,4096]{3,1,0,2:T(2,128)(2,1)}), bf16[1,2,64,4096]{3,1,0,2:T(2,128)(2,1)S(1)}, u32[]{:S(2)}, u32[]{:S(2)}) async-start(bf16[1,2,64,4096]{3,1,0,2:T(2,128)(2,1)} %copy.25), calls=%async_computation.1 | async-start | bytes 2097152 | tf_op jit(solution)/shard_map/all_to_all | solution.py:74
  53.7 37.0 %all-to-all-start = ((bf16[1,2,64,4096]{3,1,0,2:T(2,128)(2,1)}), bf16[1,2,64,4096]{3,1,0,2:T(2,128)(2,1)S(1)}, u32[]{:S(2)}, u32[]{:S(2)}) async-start(bf16[1,2,64,4096]{3,1,0,2:T(2,128)(2,1)} %copy.23), calls=%async_computation | async-start | bytes 2097152 | tf_op jit(solution)/shard_map/all_to_all | solution.py:73
  62.0 117.3 %all-gather.2.cloned.1.call-start = ((), (), s32[]{:S(2)}) async-start(), calls=%async_computation.3 | async-start | bytes 5242880 | tf_op jit(solution)/shard_map/all_gather | solution.py:85
  92.0 2.2 %copy-start.2 = (f32[256,4096]{1,0:T(8,128)S(1)}, f32[256,4096]{1,0:T(8,128)}, u32[]{:S(2)}) copy-start(f32[256,4096]{1,0:T(8,128)} %convolution_add_fusion) | copy-start | bytes 12582916
  195.0 2.2 %copy-start.3 = (bf16[1,2,1,4,512,512]{5,4,3,2,1,0:T(8,128)(2,1)S(1)}, bf16[1,2,1,4,512,512]{5,4,3,2,1,0:T(8,128)(2,1)}, u32[]{:S(2)}) copy-start(bf16[1,2,1,4,512,512]{5,4,3,2,1,0:T(8,128)(2,1)} %param.6) | copy-start | bytes 12582916
  197.2 6.0 %copy-start.1 = (s32[64]{0:T(128)S(1)}, s32[64]{0:T(128)}, u32[]{:S(2)}) copy-start(s32[64]{0:T(128)} %param.7) | copy-start | bytes 772
Sparse Core Ops, SparseCore 0:
  132.0 47.2 all-gather.1
